TPU v7x, 32 devices: a whole 2x2x4 slice. The times are simulated.
32 devices in a mesh: pair: 8 (over z, y), aux: 4 (over x, core).
Axes of the slice: x: 2, y: 2, z: 4, core: 2. Of those that a mesh axis runs over, the one named last changes fastest.
Arguments:
- x_panels: float32 [1024, 1024], P(None, 'pair'), may hold values from -0.25 to 0.25
- xbar_panels: float32 [1024, 1024], P(None, 'pair'), may hold values from -6 to 6
- bbar_below: float32 [4096, 1024], P('aux', 'pair'), may hold values from -6 to 6
- l_below: float32 [4096, 1024], P(('aux', 'pair')), may hold values from -0.09375 to 0.09375
- l_cross: float32 [512, 512], P('pair'), may hold values from -0.25 to 0.25
- dinv: float32 [2, 512, 512], P(None, 'pair'), as said below
Outputs:
- bbar_panels: float32 [1024, 1024], P(None, 'pair')
- lbar_below: float32 [4096, 1024], P(('aux', 'pair'))
- lbar_diag: float32 [2, 512, 512], P(None, 'pair')
- lbar_cross: float32 [512, 512], P('pair')
Inputs may be any that keep to these rules, and one draw needn't show every extreme that they name: Each dinv[k] is lower triangular with a positive diagonal.
All inputs are finite; a program needn't handle non-finite values.
Results may differ from a plain program's by a relative error of at most 0.00013.
Values sent between devices are 32-bit elements; how exact they have to be, the bound alone decides.
No kernel may reach another device: no remote copies, remote signals or barrier semaphores. Data moves between devices by JAX's collectives and lax.ppermute only.
A program may use at most 64 MiB of HBM per device.

v0:
```python
import jax
import jax.numpy as jnp
from jax import lax
from jax.sharding import PartitionSpec as P


def fold_with(right_side, pieces):
    return lax.dot_general(
        pieces,
        right_side,
        (((0,), (0,)), ((), ())),
        precision=lax.Precision.HIGHEST,
        preferred_element_type=jnp.float32,
    )


def body(x_panels, xbar_panels, bbar_below, l_below, l_cross, dinv):
    panel = dinv.shape[2]
    precise = lax.Precision.HIGHEST
    contract_cols = (((1,), (1,)), ((), ()))

    def below_correction(first, count):
        columns = l_below[:, first : first + count]
        folded = fold_with(bbar_below, lax.all_gather(columns, "pair", axis=0, tiled=True))
        return lax.psum(folded, "aux")

    def solve_panel(index, right_side):
        return fold_with(right_side, lax.all_gather(dinv[index], "pair", axis=0, tiled=True))

    lbar_below = lax.psum_scatter(
        -lax.dot_general(
            bbar_below,
            x_panels,
            contract_cols,
            precision=precise,
            preferred_element_type=jnp.float32,
        ),
        "pair",
        scatter_dimension=0,
        tiled=True,
    )
    late_corr = below_correction(panel, panel)
    bbar_late = solve_panel(1, xbar_panels[panel:] - late_corr)
    cross_term = fold_with(bbar_late, lax.all_gather(l_cross, "pair", axis=0, tiled=True))
    early_corr = below_correction(0, panel)
    bbar_early = solve_panel(0, xbar_panels[:panel] - early_corr - cross_term)
    x_early = x_panels[:panel]
    x_late = x_panels[panel:]
    diag_early = -lax.dot_general(
        bbar_early, x_early, contract_cols, precision=precise, preferred_element_type=jnp.float32
    )
    diag_late = -lax.dot_general(
        bbar_late, x_late, contract_cols, precision=precise, preferred_element_type=jnp.float32
    )
    cross_block = -lax.dot_general(
        bbar_late, x_early, contract_cols, precision=precise, preferred_element_type=jnp.float32
    )
    stacked = jnp.stack([diag_early, diag_late, cross_block])
    summed = lax.psum_scatter(stacked, "pair", scatter_dimension=1, tiled=True)
    bbar_panels = jnp.concatenate([bbar_early, bbar_late], axis=0)
    return (bbar_panels, lbar_below, summed[:2], summed[2])


def solution(mesh):
    in_specs = (
        P(None, "pair"),
        P(None, "pair"),
        P("aux", "pair"),
        P(("aux", "pair"), None),
        P("pair", None),
        P(None, "pair", None),
    )
    out_specs = (P(None, "pair"), P(("aux", "pair"), None), P(None, "pair", None), P("pair", None))
    return jax.shard_map(body, mesh=mesh, in_specs=in_specs, out_specs=out_specs, check_vma=False)
```

profile of v0, /device:TPU:0, one launch (start us, length us, event | category | flops | bytes accessed | tf_op | source)
XLA Modules:
  0.0 450.9 jit_solution(8527038155251425231)
XLA Ops:
  7.2 1.9 fusion.13
  10.0 1.7 fusion.14
  11.7 50.8 %all-gather.8.cloned.1.call-done = f32[1024,512]{1,0:T(8,128)} async-done(((f32[128,512]{1,0:T(8,128)}), f32[1024,512]{1,0:T(8,128)}) %all-gather.8.cloned.1.call-update) | async-done | bytes 2097168 | tf_op jit(solution)/shard_map/all_gather | solution.py:24
  62.5 5.7 %fusion.15 = f32[512,128]{1,0:T(8,128)} fusion(f32[1024,512]{1,0:T(8,128)} %all-gather.8.cloned.1.call-done, f32[1024,128]{1,0:T(8,128)S(1)} %copy-done), kind=kOutput, calls=%fused_computation.23 | convolution fusion | flops 805306368 | bytes 2883584 | tf_op jit(solution)/shard_map/dot_general | solution.py:8
  68.3 44.6 %all-gather.10.cloned.1.call-done = f32[1024,512]{1,0:T(8,128)} async-done(((f32[128,512]{1,0:T(8,128)}), f32[1024,512]{1,0:T(8,128)}) %all-gather.10.cloned.1.call-update) | async-done | bytes 2097168 | tf_op jit(solution)/shard_map/all_gather | solution.py:24
  112.9 5.7 %fusion.16 = f32[512,128]{1,0:T(8,128)} fusion(f32[1024,512]{1,0:T(8,128)} %all-gather.10.cloned.1.call-done, f32[1024,128]{1,0:T(8,128)S(1)} %copy-done), kind=kOutput, calls=%fused_computation.24 | convolution fusion | flops 805306368 | bytes 2883584 | tf_op jit(solution)/shard_map/dot_general | solution.py:8
  120.0 33.8 %all-gather.14.cloned.1.call-done = f32[1,512,512]{2,1,0:T(8,128)} async-done(((f32[1,64,512]{2,1,0:T(8,128)}), f32[1,512,512]{2,1,0:T(8,128)}) %all-gather.14.cloned.1.call-update) | async-done | bytes 1048592 | tf_op jit(solution)/shard_map/all_gather | solution.py:28
  153.9 35.1 %all-reduce.3.cloned.1.call-done = (f32[512,128]{1,0:T(8,128)}, f32[512,128]{1,0:T(8,128)}) async-done(((f32[512,128]{1,0:T(8,128)}, f32[512,128]{1,0:T(8,128)}), (f32[512,128]{1,0:T(8,128)}, f32[512,128]{1,0:T(8,128)})) %all-reduce.3.cloned.1.call-update) | async-done | bytes 524304 | tf_op jit(solution)/shard_map/psum | solution.py:25
  188.9 2.1 fusion.6
  191.0 1.0 fusion
  192.1 1.0 fusion.1
  193.1 38.2 %all-gather.12.cloned.1.call-done = f32[512,512]{1,0:T(8,128)} async-done(((f32[64,512]{1,0:T(8,128)}), f32[512,512]{1,0:T(8,128)}) %all-gather.12.cloned.1.call-update) | async-done | bytes 1048592 | tf_op jit(solution)/shard_map/all_gather | solution.py:44
  231.3 3.9 fusion.3
  235.2 37.7 %all-gather.16.cloned.1.call-done = f32[1,512,512]{2,1,0:T(8,128)} async-done(((f32[1,64,512]{2,1,0:T(8,128)}), f32[1,512,512]{2,1,0:T(8,128)}) %all-gather.16.cloned.1.call-update) | async-done | bytes 1048592 | tf_op jit(solution)/shard_map/all_gather | solution.py:28
  272.9 2.1 fusion.4
  275.7 1.0 fusion.2
  276.7 2.0 pad_maximum_fusion
  278.8 5.0 %convolution_negate_fusion = f32[1024,1024]{1,0:T(8,128)} fusion(f32[1024,128]{1,0:T(8,128)S(1)} %copy-done, f32[1024,128]{1,0:T(8,128)S(1)} %copy-done.1), kind=kOutput, calls=%fused_computation.1 | convolution fusion | flops 1611661312 | bytes 5242880 | tf_op jit(solution)/shard_map/dot_general | solution.py:31
  283.8 0.9 copy-done.3
  284.8 1.0 copy.10
  285.8 66.7 %reduce-scatter.5.cloned.1.call-done = f32[3,64,512]{2,1,0:T(8,128)} async-done(((f32[3,512,512]{2,1,0:T(8,128)}), f32[3,64,512]{2,1,0:T(8,128)}) %reduce-scatter.5.cloned.1.call-update) | async-done | bytes 393232 | tf_op jit(solution)/shard_map/reduce_scatter | solution.py:59
  352.5 1.7 slice.40
  354.1 1.6 slice_bitcast_fusion
  355.7 88.4 %reduce-scatter.3.cloned.1.call-done = f32[128,1024]{1,0:T(8,128)} async-done(((f32[1024,1024]{1,0:T(8,128)}), f32[128,1024]{1,0:T(8,128)}) %reduce-scatter.3.cloned.1.call-update) | async-done | bytes 524304 | tf_op jit(solution)/shard_map/reduce_scatter | solution.py:30
  (26 shorter events, 3.1 us)
Async XLA Ops:
  7.2 55.4 %copy-start = (f32[1024,128]{1,0:T(8,128)S(1)}, f32[1024,128]{1,0:T(8,128)}, u32[]{:S(2)}) copy-start(f32[1024,128]{1,0:T(8,128)} %param.8) | copy-start | bytes 1572868
  7.2 55.3 %all-gather.8.cloned.1.call-start = ((), (), s32[]{:S(2)}) async-start(), calls=%async_computation.2 | async-start | bytes 2359296 | tf_op jit(solution)/shard_map/all_gather | solution.py:24
  9.2 103.7 %all-gather.10.cloned.1.call-start = ((), (), s32[]{:S(2)}) async-start(), calls=%async_computation.3 | async-start | bytes 2359296 | tf_op jit(solution)/shard_map/all_gather | solution.py:24
  9.9 143.9 %all-gather.14.cloned.1.call-start = ((), (), s32[]{:S(2)}) async-start(), calls=%async_computation.7 | async-start | bytes 1179648 | tf_op jit(solution)/shard_map/all_gather | solution.py:28
  11.7 177.3 %copy-start.4 = (f32[1024,128]{1,0:T(8,128)S(1)}, f32[1024,128]{1,0:T(8,128)}, u32[]{:S(2)}) copy-start(f32[1024,128]{1,0:T(8,128)} %param.7) | copy-start | bytes 1572868
  11.7 177.3 %all-reduce.3.cloned.1.call-start = ((), (), s32[]{:S(2)}) async-start(), calls=%async_computation.9 | async-start | bytes 1048576 | tf_op jit(solution)/shard_map/psum | solution.py:25
  68.2 122.8 %copy-start.1 = (f32[1024,128]{1,0:T(8,128)S(1)}, f32[1024,128]{1,0:T(8,128)}, u32[]{:S(2)}) copy-start(f32[1024,128]{1,0:T(8,128)} %param.6) | copy-start | bytes 1572868
  118.6 112.7 %all-gather.12.cloned.1.call-start = ((), (), s32[]{:S(2)}) async-start(), calls=%async_computation.4 | async-start | bytes 1179648 | tf_op jit(solution)/shard_map/all_gather | solution.py:44
  119.2 153.7 %all-gather.16.cloned.1.call-start = ((), (), s32[]{:S(2)}) async-start(), calls=%async_computation.8 | async-start | bytes 1179648 | tf_op jit(solution)/shard_map/all_gather | solution.py:28
  119.8 232.7 %reduce-scatter.5.cloned.1.call-start = ((), (), s32[]{:S(2)}) async-start(), calls=%async_computation.6 | async-start | bytes 3538944 | tf_op jit(solution)/shard_map/reduce_scatter | solution.py:59
  275.0 0.7 copy-start.2
  278.7 165.3 %reduce-scatter.3.cloned.1.call-start = ((), (), s32[]{:S(2)}) async-start(), calls=%async_computation.5 | async-start | bytes 4718592 | tf_op jit(solution)/shard_map/reduce_scatter | solution.py:30
  283.8 1.0 copy-start.3
Sparse Core Ops, SparseCore 0:
  10.7 51.7 all-gather.7
  65.2 47.6 all-gather.9
  115.0 38.7 all-gather.13
  156.7 32.1 all-reduce.2
  190.9 40.3 all-gather.11
  233.9 38.9 all-gather.15
  278.9 73.5 reduce-scatter.4
  356.7 87.3 reduce-scatter.2
where the time goes:
time: 451 us
  waiting for transfers between devices  397 us (88%)
  matrix products  27.5 us (6%)
  between operations  14.2 us (3%)
  local copies, waits for them, and re-layouts  9.47 us (2%)
    all_gather x2, waiting for transfers between devices, below_correction(): lax.all_gather(columns, 'pair', axis=0, tiled=True)  95.4 us
    reduce_scatter x1, waiting for transfers between devices, body(): lax.psum_scatter(-lax.dot_general(bbar_below, x_panels, contract_cols, pr...  88.4 us
    all_gather x2, waiting for transfers between devices, solve_panel(): lax.all_gather(dinv[index], 'pair', axis=0, tiled=True)  71.6 us
    reduce_scatter x1, waiting for transfers between devices, body(): summed = lax.psum_scatter(stacked, 'pair', scatter_dimension=1, tiled=True)  66.7 us
    all_gather x1, waiting for transfers between devices, body(): lax.all_gather(l_cross, 'pair', axis=0, tiled=True)  38.2 us
    psum x1, waiting for transfers between devices, below_correction(): return lax.psum(folded, 'aux')  35.1 us
    dot_general x5, matrix products, fold_with(): lax.dot_general(pieces, right_side, (((0,), (0,)), ((), ())), precision=l...  19.4 us
  transfers between devices with their start and end apart: 8, of which 8 were waited for; matrix products, arithmetic and copies ran while one was open for 7% of the time, Pallas kernels for 0%

commit v1 on v0

--- a/solution.py
+++ b/solution.py
@@ -2,6 +2,23 @@
 import jax.numpy as jnp
 from jax import lax
 from jax.sharding import PartitionSpec as P
+
+
+def laid_out(tiles, dim):
+    lengths = list(tiles.shape[1:])
+    lengths[dim] *= tiles.shape[0]
+    return jnp.moveaxis(tiles, 0, dim).reshape(lengths)
+
+
+def ring_gather(shard, axis, dim):
+    size = lax.axis_size(axis)
+    right = [(i, (i + 1) % size) for i in range(size)]
+    blocks = [shard]
+    while len(blocks) < size:
+        blocks.append(lax.ppermute(blocks[-1], axis, right))
+    here = lax.axis_index(axis)
+    blocks = jnp.stack(blocks)[(here - jnp.arange(size)) % size]
+    return laid_out(blocks, dim)
 
 
 def fold_with(right_side, pieces):
@@ -41,7 +58,7 @@
     )
     late_corr = below_correction(panel, panel)
     bbar_late = solve_panel(1, xbar_panels[panel:] - late_corr)
-    cross_term = fold_with(bbar_late, lax.all_gather(l_cross, "pair", axis=0, tiled=True))
+    cross_term = fold_with(bbar_late, ring_gather(l_cross, "pair", 0))
     early_corr = below_correction(0, panel)
     bbar_early = solve_panel(0, xbar_panels[:panel] - early_corr - cross_term)
     x_early = x_panels[:panel]

time: 451 us -> 415 us (0.920)
  waiting for transfers between devices: 397 us -> 360 us
    ppermute x0 -> x7, waiting for transfers between devices: none -> 56.3 us  [ring_gather(): blocks.append(lax.ppermute(blocks[-1], axis, right))]
    all_gather x1 -> x0, waiting for transfers between devices: 38.2 us -> none  [body(): lax.all_gather(l_cross, 'pair', axis=0, tiled=True)]
    all_gather x2, waiting for transfers between devices: 71.6 us -> 35.2 us  [solve_panel(): lax.all_gather(dinv[index], 'pair', axis=0, tiled=True)]
    psum x1, waiting for transfers between devices: 35.1 us -> 16.9 us  [below_correction(): return lax.psum(folded, 'aux')]
  transfers between devices with their start and end apart: 8 -> 14, of which waited for: 8 -> 13; matrix products, arithmetic and copies ran while one was open for 7% -> 7% of each run, Pallas kernels for 0% -> 0%
where the time goes in v1:
time: 415 us; the launch traced here: 414 us
  waiting for transfers between devices  360 us (87%)
  matrix products  27.3 us (7%)
  between operations  14.3 us (3%)
  local copies, waits for them, and re-layouts  10.2 us (2%)
    all_gather x2, waiting for transfers between devices, below_correction(): lax.all_gather(columns, 'pair', axis=0, tiled=True)  95.4 us
    reduce_scatter x1, waiting for transfers between devices, body(): lax.psum_scatter(-lax.dot_general(bbar_below, x_panels, contract_cols, pr...  88.4 us
    reduce_scatter x1, waiting for transfers between devices, body(): summed = lax.psum_scatter(stacked, 'pair', scatter_dimension=1, tiled=True)  66.7 us
    ppermute x7, waiting for transfers between devices, ring_gather(): blocks.append(lax.ppermute(blocks[-1], axis, right))  56.3 us
    all_gather x2, waiting for transfers between devices, solve_panel(): lax.all_gather(dinv[index], 'pair', axis=0, tiled=True)  35.2 us
    dot_general x5, matrix products, fold_with(): lax.dot_general(pieces, right_side, (((0,), (0,)), ((), ())), precision=l...  18.2 us
    psum x1, waiting for transfers between devices, below_correction(): return lax.psum(folded, 'aux')  16.9 us
  transfers between devices with their start and end apart: 14, of which 13 were waited for; matrix products, arithmetic and copies ran while one was open for 7% of the time, Pallas kernels for 0%

profile of v1, /device:TPU:0, one launch (start us, length us, event | category | flops | bytes accessed | tf_op | source)
XLA Modules:
  0.0 414.5 jit_solution(10675080695404824150)
XLA Ops:
  7.2 1.9 fusion.14
  10.0 1.7 fusion.15
  11.7 50.8 %all-gather.7.cloned.1.call-done = f32[1024,512]{1,0:T(8,128)} async-done(((f32[128,512]{1,0:T(8,128)}), f32[1024,512]{1,0:T(8,128)}) %all-gather.7.cloned.1.call-update) | async-done | bytes 2097168 | tf_op jit(solution)/shard_map/all_gather | solution.py:41
  62.5 5.7 %fusion.16 = f32[512,128]{1,0:T(8,128)} fusion(f32[1024,512]{1,0:T(8,128)} %all-gather.7.cloned.1.call-done, f32[1024,128]{1,0:T(8,128)S(1)} %copy-done), kind=kOutput, calls=%fused_computation.38 | convolution fusion | flops 805306368 | bytes 2883584 | tf_op jit(solution)/shard_map/dot_general | solution.py:25
  68.2 44.6 %all-gather.9.cloned.1.call-done = f32[1024,512]{1,0:T(8,128)} async-done(((f32[128,512]{1,0:T(8,128)}), f32[1024,512]{1,0:T(8,128)}) %all-gather.9.cloned.1.call-update) | async-done | bytes 2097168 | tf_op jit(solution)/shard_map/all_gather | solution.py:41
  112.9 5.7 %fusion.17 = f32[512,128]{1,0:T(8,128)} fusion(f32[1024,512]{1,0:T(8,128)} %all-gather.9.cloned.1.call-done, f32[1024,128]{1,0:T(8,128)S(1)} %copy-done), kind=kOutput, calls=%fused_computation.39 | convolution fusion | flops 805306368 | bytes 2883584 | tf_op jit(solution)/shard_map/dot_general | solution.py:25
  119.4 7.1 %collective-permute-done = f32[64,512]{1,0:T(8,128)S(1)} collective-permute-done((f32[64,512]{1,0:T(8,128)S(1)}, f32[64,512]{1,0:T(8,128)S(1)}, u32[]{:S(2)}, u32[]{:S(2)}) %collective-permute-start) | collective-permute-done | bytes 131104 | tf_op jit(solution)/shard_map/ppermute | solution.py:18
  126.6 7.9 %collective-permute-done.1 = f32[64,512]{1,0:T(8,128)S(1)} collective-permute-done((f32[64,512]{1,0:T(8,128)S(1)}, f32[64,512]{1,0:T(8,128)S(1)}, u32[]{:S(2)}, u32[]{:S(2)}) %collective-permute-start.1) | collective-permute-done | bytes 131104 | tf_op jit(solution)/shard_map/ppermute | solution.py:18
  134.5 7.9 %collective-permute-done.2 = f32[64,512]{1,0:T(8,128)S(1)} collective-permute-done((f32[64,512]{1,0:T(8,128)S(1)}, f32[64,512]{1,0:T(8,128)S(1)}, u32[]{:S(2)}, u32[]{:S(2)}) %collective-permute-start.2) | collective-permute-done | bytes 131104 | tf_op jit(solution)/shard_map/ppermute | solution.py:18
  142.4 9.9 %collective-permute-done.3 = f32[64,512]{1,0:T(8,128)S(1)} collective-permute-done((f32[64,512]{1,0:T(8,128)S(1)}, f32[64,512]{1,0:T(8,128)S(1)}, u32[]{:S(2)}, u32[]{:S(2)}) %collective-permute-start.3) | collective-permute-done | bytes 131104 | tf_op jit(solution)/shard_map/ppermute | solution.py:18
  152.3 8.2 %collective-permute-done.4 = f32[64,512]{1,0:T(8,128)S(1)} collective-permute-done((f32[64,512]{1,0:T(8,128)S(1)}, f32[64,512]{1,0:T(8,128)S(1)}, u32[]{:S(2)}, u32[]{:S(2)}) %collective-permute-start.4) | collective-permute-done | bytes 131104 | tf_op jit(solution)/shard_map/ppermute | solution.py:18
  160.5 7.6 %collective-permute-done.5 = f32[64,512]{1,0:T(8,128)S(1)} collective-permute-done((f32[64,512]{1,0:T(8,128)S(1)}, f32[64,512]{1,0:T(8,128)S(1)}, u32[]{:S(2)}, u32[]{:S(2)}) %collective-permute-start.5) | collective-permute-done | bytes 131104 | tf_op jit(solution)/shard_map/ppermute | solution.py:18
  168.2 7.6 %collective-permute-done.6 = f32[64,512]{1,0:T(8,128)S(1)} collective-permute-done((f32[64,512]{1,0:T(8,128)S(1)}, f32[64,512]{1,0:T(8,128)S(1)}, u32[]{:S(2)}, u32[]{:S(2)}) %collective-permute-start.6) | collective-permute-done | bytes 131104 | tf_op jit(solution)/shard_map/ppermute | solution.py:18
  176.5 16.9 %all-reduce.3.cloned.1.call-done = (f32[512,128]{1,0:T(8,128)}, f32[512,128]{1,0:T(8,128)}) async-done(((f32[512,128]{1,0:T(8,128)}, f32[512,128]{1,0:T(8,128)}), (f32[512,128]{1,0:T(8,128)}, f32[512,128]{1,0:T(8,128)})) %all-reduce.3.cloned.1.call-update) | async-done | bytes 524304 | tf_op jit(solution)/shard_map/psum | solution.py:42
  193.4 2.2 fusion.5
  196.7 2.0 fusion.1
  198.7 2.5 convolution_subtract_fusion
  201.2 35.2 %all-gather.13.cloned.1.call-done = f32[1,512,512]{2,1,0:T(8,128)} async-done(((f32[1,64,512]{2,1,0:T(8,128)}), f32[1,512,512]{2,1,0:T(8,128)}) %all-gather.13.cloned.1.call-update) | async-done | bytes 1048592 | tf_op jit(solution)/shard_map/all_gather | solution.py:45
  236.4 2.1 fusion.3
  240.2 2.0 pad_maximum_fusion
  242.2 5.0 %convolution_negate_fusion = f32[1024,1024]{1,0:T(8,128)} fusion(f32[1024,128]{1,0:T(8,128)S(1)} %copy-done, f32[1024,128]{1,0:T(8,128)S(1)} %copy-done.2), kind=kOutput, calls=%fused_computation.2 | convolution fusion | flops 1611661312 | bytes 5242880 | tf_op jit(solution)/shard_map/dot_general | solution.py:48
  249.3 66.7 %reduce-scatter.5.cloned.1.call-done = f32[3,64,512]{2,1,0:T(8,128)} async-done(((f32[3,512,512]{2,1,0:T(8,128)}), f32[3,64,512]{2,1,0:T(8,128)}) %reduce-scatter.5.cloned.1.call-update) | async-done | bytes 393232 | tf_op jit(solution)/shard_map/reduce_scatter | solution.py:76
  316.0 1.7 slice.42
  319.2 88.4 %reduce-scatter.3.cloned.1.call-done = f32[128,1024]{1,0:T(8,128)} async-done(((f32[1024,1024]{1,0:T(8,128)}), f32[128,1024]{1,0:T(8,128)}) %reduce-scatter.3.cloned.1.call-update) | async-done | bytes 524304 | tf_op jit(solution)/shard_map/reduce_scatter | solution.py:47
  (54 shorter events, 8.8 us)
Async XLA Ops:
  7.2 55.4 %copy-start = (f32[1024,128]{1,0:T(8,128)S(1)}, f32[1024,128]{1,0:T(8,128)}, u32[]{:S(2)}) copy-start(f32[1024,128]{1,0:T(8,128)} %param.8) | copy-start | bytes 1572868
  7.2 55.3 %all-gather.7.cloned.1.call-start = ((), (), s32[]{:S(2)}) async-start(), calls=%async_computation.2 | async-start | bytes 2359296 | tf_op jit(solution)/shard_map/all_gather | solution.py:41
  9.2 103.7 %all-gather.9.cloned.1.call-start = ((), (), s32[]{:S(2)}) async-start(), calls=%async_computation.3 | async-start | bytes 2359296 | tf_op jit(solution)/shard_map/all_gather | solution.py:41
  9.9 166.6 %all-gather.11.cloned.1.call-start = ((), (), s32[]{:S(2)}) async-start(), calls=%async_computation.6 | async-start | bytes 1179648 | tf_op jit(solution)/shard_map/all_gather | solution.py:45
  11.7 107.0 %copy-start.7 = (f32[64,512]{1,0:T(8,128)S(1)}, f32[64,512]{1,0:T(8,128)}, u32[]{:S(2)}) copy-start(f32[64,512]{1,0:T(8,128)} %param.10) | copy-start | bytes 393220
  11.7 181.7 %all-reduce.3.cloned.1.call-start = ((), (), s32[]{:S(2)}) async-start(), calls=%async_computation.8 | async-start | bytes 1048576 | tf_op jit(solution)/shard_map/psum | solution.py:42
  118.6 77.0 %copy-start.2 = (f32[1024,128]{1,0:T(8,128)S(1)}, f32[1024,128]{1,0:T(8,128)}, u32[]{:S(2)}) copy-start(f32[1024,128]{1,0:T(8,128)} %param.6) | copy-start | bytes 1572868
  118.6 117.7 %all-gather.13.cloned.1.call-start = ((), (), s32[]{:S(2)}) async-start(), calls=%async_computation.7 | async-start | bytes 1179648 | tf_op jit(solution)/shard_map/all_gather | solution.py:45
  118.7 7.8 %collective-permute-start = (f32[64,512]{1,0:T(8,128)S(1)}, f32[64,512]{1,0:T(8,128)S(1)}, u32[]{:S(2)}, u32[]{:S(2)}) collective-permute-start(f32[64,512]{1,0:T(8,128)S(1)} %copy-done.7), channel_id=1, source_target_pairs={{0,4},{4,8},{8,12},{12,16},{16,20},{20,24},{24,28},{28,0},{1,5},{5... | collective-permute-start | bytes 393224 | tf_op jit(solution)/shard_map/ppermute | solution.py:18
  119.3 196.6 %reduce-scatter.5.cloned.1.call-start = ((), (), s32[]{:S(2)}) async-start(), calls=%async_computation.5 | async-start | bytes 3538944 | tf_op jit(solution)/shard_map/reduce_scatter | solution.py:76
  126.5 7.9 %collective-permute-start.1 = (f32[64,512]{1,0:T(8,128)S(1)}, f32[64,512]{1,0:T(8,128)S(1)}, u32[]{:S(2)}, u32[]{:S(2)}) collective-permute-start(f32[64,512]{1,0:T(8,128)S(1)} %collective-permute-done), channel_id=1, source_target_pairs={{0,4},{4,8},{8,12},{12,16},{16,20},{20,24},{24,28},{28,0},{1,5},{5... | collective-permute-start | bytes 393224 | tf_op jit(solution)/shard_map/ppermute | solution.py:18
  134.4 7.9 %collective-permute-start.2 = (f32[64,512]{1,0:T(8,128)S(1)}, f32[64,512]{1,0:T(8,128)S(1)}, u32[]{:S(2)}, u32[]{:S(2)}) collective-permute-start(f32[64,512]{1,0:T(8,128)S(1)} %collective-permute-done.1), channel_id=1, source_target_pairs={{0,4},{4,8},{8,12},{12,16},{16,20},{20,24},{24,28},{28,0},{1,5},{5... | collective-permute-start | bytes 393224 | tf_op jit(solution)/shard_map/ppermute | solution.py:18
  142.4 9.9 %collective-permute-start.3 = (f32[64,512]{1,0:T(8,128)S(1)}, f32[64,512]{1,0:T(8,128)S(1)}, u32[]{:S(2)}, u32[]{:S(2)}) collective-permute-start(f32[64,512]{1,0:T(8,128)S(1)} %collective-permute-done.2), channel_id=1, source_target_pairs={{0,4},{4,8},{8,12},{12,16},{16,20},{20,24},{24,28},{28,0},{1,5},{5... | collective-permute-start | bytes 393224 | tf_op jit(solution)/shard_map/ppermute | solution.py:18
  152.3 8.2 %collective-permute-start.4 = (f32[64,512]{1,0:T(8,128)S(1)}, f32[64,512]{1,0:T(8,128)S(1)}, u32[]{:S(2)}, u32[]{:S(2)}) collective-permute-start(f32[64,512]{1,0:T(8,128)S(1)} %collective-permute-done.3), channel_id=1, source_target_pairs={{0,4},{4,8},{8,12},{12,16},{16,20},{20,24},{24,28},{28,0},{1,5},{5... | collective-permute-start | bytes 393224 | tf_op jit(solution)/shard_map/ppermute | solution.py:18
  160.5 7.7 %collective-permute-start.5 = (f32[64,512]{1,0:T(8,128)S(1)}, f32[64,512]{1,0:T(8,128)S(1)}, u32[]{:S(2)}, u32[]{:S(2)}) collective-permute-start(f32[64,512]{1,0:T(8,128)S(1)} %collective-permute-done.4), channel_id=1, source_target_pairs={{0,4},{4,8},{8,12},{12,16},{16,20},{20,24},{24,28},{28,0},{1,5},{5... | collective-permute-start | bytes 393224 | tf_op jit(solution)/shard_map/ppermute | solution.py:18
  168.2 7.7 %collective-permute-start.6 = (f32[64,512]{1,0:T(8,128)S(1)}, f32[64,512]{1,0:T(8,128)S(1)}, u32[]{:S(2)}, u32[]{:S(2)}) collective-permute-start(f32[64,512]{1,0:T(8,128)S(1)} %collective-permute-done.5), channel_id=1, source_target_pairs={{0,4},{4,8},{8,12},{12,16},{16,20},{20,24},{24,28},{28,0},{1,5},{5... | collective-permute-start | bytes 393224 | tf_op jit(solution)/shard_map/ppermute | solution.py:18
  193.4 5.3 %copy-start.5 = (f32[1024,128]{1,0:T(8,128)S(1)}, f32[1024,128]{1,0:T(8,128)}, u32[]{:S(2)}) copy-start(f32[1024,128]{1,0:T(8,128)} %param.7) | copy-start | bytes 1572868
  193.4 5.3 %copy-start.6 = (f32[512,128]{1,0:T(8,128)S(1)}, f32[512,128]{1,0:T(8,128)}, u32[]{:S(2)}) copy-start(f32[512,128]{1,0:T(8,128)} %get-tuple-element.9) | copy-start | bytes 786436
  201.2 39.0 %copy-start.1 = (f32[1,512,512]{2,1,0:T(8,128)S(1)}, f32[1,512,512]{2,1,0:T(8,128)}, u32[]{:S(2)}) copy-start(f32[1,512,512]{2,1,0:T(8,128)} %fusion.1) | copy-start | bytes 3145732
  238.5 0.7 copy-start.3
  242.2 165.4 %reduce-scatter.3.cloned.1.call-start = ((), (), s32[]{:S(2)}) async-start(), calls=%async_computation.4 | async-start | bytes 4718592 | tf_op jit(solution)/shard_map/reduce_scatter | solution.py:47
  247.3 1.0 copy-start.4
Sparse Core Ops, SparseCore 0:
  10.7 51.7 all-gather.6
  65.2 47.6 all-gather.8
  115.0 41.4 all-gather.10
  159.4 33.9 all-reduce.2
  195.9 40.3 all-gather.12
  242.3 73.5 reduce-scatter.4
  320.2 87.4 reduce-scatter.2
